TPU v7x, 256 devices: a whole 4x4x8 slice. The times are simulated.
256 devices in a mesh: row: 32 (over z, y_hi, core), col: 8 (over x, y_lo).
Axes of the slice: x: 4, y: 4 (y_hi: 2, y_lo: 2; y = y_hi * 2 + y_lo), z: 8, core: 2. Of those that a mesh axis runs over, the one named last changes fastest.
Arguments:
- feature_map: bfloat16 [256, 256, 384], P('row', 'col'), may hold values from -6 to 6
- kernel: float32 [7, 7, 384], replicated, may hold values from -0.875 to 0.875
- ln_gain: float32 [384], replicated, may hold values from 0.5 to 1.5
- ln_bias: float32 [384], replicated, may hold values from -3 to 3
- w_in: bfloat16 [384, 1536], P(None, ('row', 'col')), may hold values from -0.3125 to 0.3125
- b_in: float32 [1536], replicated, may hold values from -3 to 3
- w_out: bfloat16 [1536, 384], P(('row', 'col')), may hold values from -0.15625 to 0.15625
- b_out: float32 [384], replicated, may hold values from -3 to 3
- layer_scale: float32 [384], replicated, may hold values from 0.5 to 1.5
- cotangent: bfloat16 [256, 256, 384], P('row', 'col'), may hold values from -6 to 6
Outputs:
- block_out: bfloat16 [256, 256, 384], P('row', 'col')
- grad_input: bfloat16 [256, 256, 384], P('row', 'col')
- grad_w_in: float32 [384, 1536], P(None, ('row', 'col'))
- grad_w_out: float32 [1536, 384], P(('row', 'col'))
- small_grads: float32 [53, 384], replicated
- grad_b_in: float32 [1536], replicated
All inputs are finite; a program needn't handle non-finite values.
Results may differ from a plain program's by a relative error of at most 0.007.
Values may be sent and summed in bfloat16 or wider, within the bound.
No kernel may reach another device: no remote copies, remote signals or barrier semaphores. Data moves between devices by JAX's collectives and lax.ppermute only.
A program may use at most 64 MiB of HBM per device.

v0:
```python
import math
import jax
import jax.numpy as jnp
from jax import lax
from jax.sharding import PartitionSpec as P


def padded_2(x, sides, width):
    for axis, dim in sides:
        peers, length = (lax.axis_size(axis), x.shape[dim])
        up = [(i, (i + 1) % peers) for i in range(peers - 1)]
        down = [(j, i) for i, j in up]
        last = lax.slice_in_dim(x, length - width, length, axis=dim)
        first = lax.slice_in_dim(x, 0, width, axis=dim)
        before = lax.ppermute(last, axis, up)
        after = lax.ppermute(first, axis, down)
        x = jnp.concatenate([before, x, after], axis=dim)
    return x


def gelu_parts(hidden):
    normal_cdf = 0.5 * (1.0 + jax.scipy.special.erf(hidden * (1.0 / math.sqrt(2.0))))
    density = jnp.exp(-0.5 * hidden * hidden) * (1.0 / math.sqrt(2.0 * math.pi))
    return (hidden * normal_cdf, normal_cdf + hidden * density)


def extend(field):
    return padded_2(field, (("row", 0), ("col", 1)), 3)


def on_device(
    feature_map, kernel, ln_gain, ln_bias, w_in, b_in, w_out, b_out, layer_scale, cotangent
):
    row_count, col_count, channels = feature_map.shape
    pixels = row_count * col_count
    padded = extend(feature_map).astype(jnp.float32)
    conv = jnp.zeros((row_count, col_count, channels), jnp.float32)
    for tap_row in range(7):
        for tap_col in range(7):
            conv = (
                conv
                + padded[tap_row : tap_row + row_count, tap_col : tap_col + col_count]
                * kernel[tap_row, tap_col]
            )
    average = jnp.mean(conv, -1, keepdims=True)
    centered = conv - average
    variance = jnp.mean(centered * centered, -1, keepdims=True)
    inv_std = lax.rsqrt(variance + 1e-06)
    unit_scaled = centered * inv_std
    normed = (unit_scaled * ln_gain + ln_bias).astype(jnp.bfloat16).reshape(pixels, channels)
    contract_last = (((1,), (1,)), ((), ()))
    contract_first = (((0,), (0,)), ((), ()))
    w_in_full = lax.all_gather(w_in, ("row", "col"), axis=1, tiled=True)
    w_out_full = lax.all_gather(w_out, ("row", "col"), axis=0, tiled=True)
    hidden = jnp.dot(normed, w_in_full, preferred_element_type=jnp.float32) + b_in
    act_value, slope = gelu_parts(hidden)
    activated = act_value.astype(jnp.bfloat16)
    mixed = jnp.dot(activated, w_out_full, preferred_element_type=jnp.float32) + b_out
    source = feature_map.astype(jnp.float32).reshape(pixels, channels)
    block_out = (
        (source + layer_scale * mixed).astype(jnp.bfloat16).reshape(row_count, col_count, channels)
    )
    grad_flow = cotangent.astype(jnp.float32).reshape(pixels, channels)
    grad_mixed = grad_flow * layer_scale
    mixed_low = grad_mixed.astype(jnp.bfloat16)
    grad_act = lax.dot_general(
        mixed_low, w_out_full, contract_last, preferred_element_type=jnp.float32
    )
    grad_hidden = (grad_act * slope).astype(jnp.bfloat16)
    grad_w_out = lax.psum_scatter(
        lax.dot_general(activated, mixed_low, contract_first, preferred_element_type=jnp.float32),
        ("row", "col"),
        scatter_dimension=0,
        tiled=True,
    )
    win_term = lax.dot_general(
        normed, grad_hidden, contract_first, preferred_element_type=jnp.float32
    )
    grad_w_in = lax.psum_scatter(win_term, ("row", "col"), scatter_dimension=1, tiled=True)
    grad_normed = lax.dot_general(
        grad_hidden, w_in_full, contract_last, preferred_element_type=jnp.float32
    )
    grad_normed = grad_normed.reshape(row_count, col_count, channels)
    grad_gain = jnp.sum(grad_normed * unit_scaled, (0, 1))
    grad_lnb = jnp.sum(grad_normed, (0, 1))
    scaled_grad = grad_normed * ln_gain
    grad_conv = inv_std * (
        scaled_grad
        - jnp.mean(scaled_grad, -1, keepdims=True)
        - unit_scaled * jnp.mean(scaled_grad * unit_scaled, -1, keepdims=True)
    )
    tap_terms = []
    for tap_row in range(7):
        for tap_col in range(7):
            tap_terms.append(
                jnp.sum(
                    padded[tap_row : tap_row + row_count, tap_col : tap_col + col_count]
                    * grad_conv,
                    (0, 1),
                )
            )
    grad_pad = extend(grad_conv.astype(jnp.bfloat16)).astype(jnp.float32)
    back_conv = jnp.zeros((row_count, col_count, channels), jnp.float32)
    for tap_row in range(7):
        for tap_col in range(7):
            back_conv = (
                back_conv
                + grad_pad[
                    6 - tap_row : 6 - tap_row + row_count, 6 - tap_col : 6 - tap_col + col_count
                ]
                * kernel[tap_row, tap_col]
            )
    grad_input = (cotangent.astype(jnp.float32) + back_conv).astype(jnp.bfloat16)
    small_local = jnp.concatenate(
        [
            jnp.stack(tap_terms, 0),
            grad_gain[None],
            grad_lnb[None],
            jnp.sum(grad_mixed, 0)[None],
            jnp.sum(grad_flow * mixed, 0)[None],
        ],
        0,
    )
    bias_local = jnp.sum(grad_hidden.astype(jnp.float32), 0)
    small_grads, grad_b_in = lax.psum((small_local, bias_local), ("row", "col"))
    return (block_out, grad_input, grad_w_in, grad_w_out, small_grads, grad_b_in)


def solution(mesh):
    placed = (
        P("row", "col", None),
        P(),
        P(),
        P(),
        P(None, ("row", "col")),
        P(),
        P(("row", "col"), None),
        P(),
        P(),
        P("row", "col", None),
    )
    return jax.shard_map(
        on_device,
        mesh=mesh,
        in_specs=placed,
        out_specs=(
            P("row", "col", None),
            P("row", "col", None),
            P(None, ("row", "col")),
            P(("row", "col"), None),
            P(),
            P(),
        ),
        check_vma=False,
    )
```

profile of v0, /device:TPU:99, one launch (start us, length us, event | category | flops | bytes accessed | tf_op | source)
XLA Modules:
  0.0 1693.0 jit_solution(1590831697639832717)
XLA Ops:
  7.2 0.0 all-gather.5.cloned.1.call-start
  7.2 0.7 all-gather.5.cloned.1.call-update
  7.9 0.0 all-gather.7.cloned.1.call-start
  7.9 0.9 fusion.63
  8.9 5.4 collective-permute-start
  14.3 1.9 collective-permute-start.1
  16.2 0.0 all-gather.7.cloned.1.call-update
  16.2 0.0 all-reduce.5.cloned.1.call-start
  16.3 1.1 slice_reduce_fusion.47
  17.4 1.0 fusion.56
  18.4 1.2 slice_reduce_fusion.48
  19.6 0.0 copy-start.5
  19.7 0.0 collective-permute-done
  19.7 1.0 constant_dynamic-update-slice_fusion.1
  20.7 0.8 collective-permute-done.1
  21.5 2.3 collective-permute-start.3
  23.8 3.0 collective-permute-start.2
  26.8 1.0 slice_reduce_fusion.46
  27.9 0.0 copy-start.35
  27.9 0.0 copy-start.37
  27.9 0.6 broadcast_in_dim.10
  28.5 0.0 collective-permute-done.3
  28.5 1.0 collective-permute-done.2
  29.5 0.1 maximum_convert_fusion
  29.6 0.0 copy-start.39
  29.6 0.0 copy-start.42
  29.6 3.2 fusion.60
  32.9 0.2 multiply_reduce_fusion.52
  33.2 0.1 add_convert_fusion
  33.3 671.1 %all-gather.5.cloned.1.call-done = bf16[256,6,384]{2,1,0:T(8,128)(2,1)} async-done(((bf16[1,6,384]{2,1,0:T(8,128)(2,1)}), bf16[256,6,384]{2,1,0:T(8,128)(2,1)}) %all-gather.5.cloned.1.call-update) | async-done | bytes 1179664 | tf_op jit(solution)/shard_map/all_gather | solution.py:53
  704.4 2.3 reshape.74
  706.7 2.5 multiply_convert_fusion
  709.2 684.3 %all-gather.7.cloned.1.call-done = bf16[256,6,384]{2,1,0:T(8,128)(2,1)} async-done(((bf16[1,6,384]{2,1,0:T(8,128)(2,1)}), bf16[256,6,384]{2,1,0:T(8,128)(2,1)}) %all-gather.7.cloned.1.call-update) | async-done | bytes 1179664 | tf_op jit(solution)/shard_map/all_gather | solution.py:54
  1393.6 3.3 reshape.76
  1396.8 3.5 fusion.58
  1400.3 0.9 convert_reduce_fusion
  1401.3 0.7 fusion.59
  1401.9 2.0 fusion.64
  1404.0 2.1 fusion.65
  1406.1 0.2 multiply_reduce_fusion
  1406.3 0.1 div.17
  1406.4 0.9 multiply_reduce_fusion.1
  1407.3 0.7 multiply_reduce_fusion.19
  1408.1 0.0 copy-start.41
  1408.1 0.6 multiply_reduce_fusion.37
  1409.2 4.4 concatenate.19
  1413.6 0.0 all-reduce.5.cloned.1.call-update
  1413.6 0.0 copy-start.4
  1413.6 0.0 copy-start.6
  1413.8 0.0 copy-start.36
  1413.8 0.0 copy-start.38
  1413.8 1.9 collective-permute-start.5
  1415.7 5.1 collective-permute-start.4
  1420.9 0.5 collective-permute-done.5
  1421.4 0.9 collective-permute-done.4
  1422.3 1.9 collective-permute-start.7
  1424.3 3.4 collective-permute-start.6
  1427.6 73.7 %psum.15 = f32[1536]{0:T(1024)} all-reduce(f32[1536]{0:T(1024)S(1)} %get-tuple-element.129), channel_id=1, replica_groups=mesh['row'=32,'col'=8] {'row','col'}, use_global_device_ids=true, to_apply=%region_61.0 | all-reduce | flops 1536 | bytes 12288 | tf_op jit(solution)/shard_map/psum | solution.py:125
  1501.3 0.1 maximum_convert_fusion.1
  1501.7 3.5 fusion.7
  1505.2 177.1 %all-reduce.5.cloned.1.call-done = (f32[384,1536]{0,1:T(8,128)}, f32[1536,384]{1,0:T(8,128)}, f32[53,384]{1,0:T(8,128)}) async-done(((f32[384,1536]{0,1:T(8,128)}, f32[1536,384]{1,0:T(8,128)}, f32[53,384]{1,0:T(8,128)}), (f32[384,1536]{0,1:T(8,128)}, f32[1536,384]{1,0:T(8,128)}, f32[53,384]{1,0:T(8,128)})) %all-reduce.5.cloned.1.call-update) | async-done | bytes 4800016
  1682.2 1.3 constant_dynamic-slice_fusion.1
  1683.6 1.3 constant_dynamic-slice_fusion
  1684.9 1.5 copy.21
  (141 shorter events, 0.5 us)
Async XLA Ops:
  7.2 697.2 %all-gather.5.cloned.1.call-start = ((), (), s32[]{:S(2)}) async-start(), calls=%async_computation | async-start | bytes 1579008 | tf_op jit(solution)/shard_map/all_gather | solution.py:53
  7.9 1385.7 %all-gather.7.cloned.1.call-start = ((), (), s32[]{:S(2)}) async-start(), calls=%async_computation.1 | async-start | bytes 1579008 | tf_op jit(solution)/shard_map/all_gather | solution.py:54
  8.9 10.8 collective-permute-start
  14.3 7.2 collective-permute-start.1
  16.2 1666.0 %all-reduce.5.cloned.1.call-start = ((), (), s32[]{:S(2)}) async-start(), calls=%async_computation.2 | async-start | bytes 9609216
  19.6 13.2 copy-start.5
  19.6 13.1 copy-start.7
  19.7 13.1 copy-start.9
  19.7 13.1 copy-start.11
  19.7 13.1 copy-start.13
  19.7 13.1 copy-start.15
  21.5 6.9 collective-permute-start.3
  23.8 5.7 collective-permute-start.2
  27.8 5.0 copy-start.17
  27.8 5.0 copy-start.19
  27.8 5.0 copy-start.21
  27.8 5.0 copy-start.23
  27.8 5.0 copy-start.25
  27.8 5.0 copy-start.27
  27.8 5.0 copy-start.29
  27.8 5.0 copy-start.31
  27.9 5.0 copy-start.33
  27.9 5.0 copy-start.35
  27.9 5.0 copy-start.37
  29.6 3.5 copy-start.39
  29.6 3.5 copy-start.42
  709.2 691.1 %copy-start = (bf16[256,1536]{1,0:T(8,128)(2,1)}, bf16[256,1536]{1,0:T(8,128)(2,1)S(1)}, u32[]{:S(2)}) copy-start(bf16[256,1536]{1,0:T(8,128)(2,1)S(1)} %get-tuple-element.126) | copy-start | bytes 2359300
  1396.8 3.5 copy-start.2
  1396.8 3.5 copy-start.3
  1400.3 0.9 copy-start.40
  1401.9 2.0 copy-start.1
  1408.0 1.1 copy-start.43
  1408.1 1.2 copy-start.41
  1413.6 87.9 %copy-start.4 = (bf16[8,32,384]{2,1,0:T(8,128)(2,1)S(1)}, bf16[8,32,384]{2,1,0:T(8,128)(2,1)}, u32[]{:S(2)}) copy-start(bf16[8,32,384]{2,1,0:T(8,128)(2,1)} %param.19) | copy-start | bytes 589828
  1413.6 87.9 %copy-start.6 = (f32[384]{0:T(512)S(1)}, f32[384]{0:T(512)}, u32[]{:S(2)}) copy-start(f32[384]{0:T(512)} %copy-done.5) | copy-start | bytes 4612
  1413.6 87.9 %copy-start.8 = (f32[384]{0:T(512)S(1)}, f32[384]{0:T(512)}, u32[]{:S(2)}) copy-start(f32[384]{0:T(512)} %copy-done.7) | copy-start | bytes 4612
  1413.6 87.9 %copy-start.10 = (f32[384]{0:T(512)S(1)}, f32[384]{0:T(512)}, u32[]{:S(2)}) copy-start(f32[384]{0:T(512)} %copy-done.9) | copy-start | bytes 4612
  1413.6 87.9 %copy-start.12 = (f32[384]{0:T(512)S(1)}, f32[384]{0:T(512)}, u32[]{:S(2)}) copy-start(f32[384]{0:T(512)} %copy-done.11) | copy-start | bytes 4612
  1413.7 87.9 %copy-start.14 = (f32[384]{0:T(512)S(1)}, f32[384]{0:T(512)}, u32[]{:S(2)}) copy-start(f32[384]{0:T(512)} %copy-done.13) | copy-start | bytes 4612
  1413.7 87.9 %copy-start.16 = (f32[384]{0:T(512)S(1)}, f32[384]{0:T(512)}, u32[]{:S(2)}) copy-start(f32[384]{0:T(512)} %copy-done.15) | copy-start | bytes 4612
  1413.7 87.9 %copy-start.18 = (f32[384]{0:T(512)S(1)}, f32[384]{0:T(512)}, u32[]{:S(2)}) copy-start(f32[384]{0:T(512)} %copy-done.17) | copy-start | bytes 4612
  1413.7 87.9 %copy-start.20 = (f32[384]{0:T(512)S(1)}, f32[384]{0:T(512)}, u32[]{:S(2)}) copy-start(f32[384]{0:T(512)} %copy-done.19) | copy-start | bytes 4612
  1413.7 87.9 %copy-start.22 = (f32[384]{0:T(512)S(1)}, f32[384]{0:T(512)}, u32[]{:S(2)}) copy-start(f32[384]{0:T(512)} %copy-done.21) | copy-start | bytes 4612
  1413.7 87.9 %copy-start.24 = (f32[384]{0:T(512)S(1)}, f32[384]{0:T(512)}, u32[]{:S(2)}) copy-start(f32[384]{0:T(512)} %copy-done.23) | copy-start | bytes 4612
  1413.7 87.9 %copy-start.26 = (f32[384]{0:T(512)S(1)}, f32[384]{0:T(512)}, u32[]{:S(2)}) copy-start(f32[384]{0:T(512)} %copy-done.25) | copy-start | bytes 4612
  1413.7 87.9 %copy-start.28 = (f32[384]{0:T(512)S(1)}, f32[384]{0:T(512)}, u32[]{:S(2)}) copy-start(f32[384]{0:T(512)} %copy-done.27) | copy-start | bytes 4612
  1413.7 87.9 %copy-start.30 = (f32[384]{0:T(512)S(1)}, f32[384]{0:T(512)}, u32[]{:S(2)}) copy-start(f32[384]{0:T(512)} %copy-done.29) | copy-start | bytes 4612
  1413.7 87.9 %copy-start.32 = (f32[384]{0:T(512)S(1)}, f32[384]{0:T(512)}, u32[]{:S(2)}) copy-start(f32[384]{0:T(512)} %copy-done.31) | copy-start | bytes 4612
  1413.8 87.9 %copy-start.34 = (f32[384]{0:T(512)S(1)}, f32[384]{0:T(512)}, u32[]{:S(2)}) copy-start(f32[384]{0:T(512)} %copy-done.33) | copy-start | bytes 4612
  1413.8 87.9 %copy-start.36 = (f32[384]{0:T(512)S(1)}, f32[384]{0:T(512)}, u32[]{:S(2)}) copy-start(f32[384]{0:T(512)} %copy-done.35) | copy-start | bytes 4612
  1413.8 87.9 %copy-start.38 = (f32[384]{0:T(512)S(1)}, f32[384]{0:T(512)}, u32[]{:S(2)}) copy-start(f32[384]{0:T(512)} %copy-done.37) | copy-start | bytes 4612
  1413.8 7.6 collective-permute-start.5
  1415.7 6.5 collective-permute-start.4
  1422.3 79.0 %collective-permute-start.7 = (bf16[14,3,384]{2,1,0:T(4,128)(2,1)S(1)}, bf16[14,3,384]{2,1,0:T(4,128)(2,1)S(1)}, u32[]{:S(2)}, u32[]{:S(2)}) collective-permute-start(bf16[14,3,384]{2,1,0:T(4,128)(2,1)S(1)} %get-tuple-element.118), channel_id=1, source_target_pairs={{1,0},{2,1},{3,2},{4,3},{5,4},{6,5},{7,6},{9,8},{10,9},{11,10},{12... | collective-permute-start | bytes 96776 | tf_op jit(solution)/shard_map/ppermute | solution.py:16
  1424.3 77.1 %collective-permute-start.6 = (bf16[14,3,384]{2,1,0:T(4,128)(2,1)S(1)}, bf16[14,3,384]{2,1,0:T(4,128)(2,1)S(1)}, u32[]{:S(2)}, u32[]{:S(2)}) collective-permute-start(bf16[14,3,384]{2,1,0:T(4,128)(2,1)S(1)} %get-tuple-element.117), channel_id=1, source_target_pairs={{0,1},{1,2},{2,3},{3,4},{4,5},{5,6},{6,7},{8,9},{9,10},{10,11},{11... | collective-permute-start | bytes 96776 | tf_op jit(solution)/shard_map/ppermute | solution.py:15
Sparse Core Ops, SparseCore 0:
  9.9 694.4 all-gather.4
  706.3 687.2 all-gather.6
  1413.7 268.4 all-reduce.4
where the time goes:
time: 1690 us
  waiting for transfers between devices  1540 us (91%)
  blocking collectives  73.7 us (4%)
  starting transfers between devices  25.1 us (1%)
  local copies, waits for them, and re-layouts  20.5 us (1%)
    all_gather x1, waiting for transfers between devices, on_device(): w_out_full = lax.all_gather(w_out, ('row', 'col'), axis=0, tiled=True)  684 us
    all_gather x1, waiting for transfers between devices, on_device(): w_in_full = lax.all_gather(w_in, ('row', 'col'), axis=1, tiled=True)  671 us
    unnamed x4, waiting for transfers between devices  178 us
    psum x1, blocking collectives, on_device(): small_grads, grad_b_in = lax.psum((small_local, bias_local), ('row', 'col'))  73.7 us
  transfers between devices with their start and end apart: 11, of which 7 were waited for; matrix products, arithmetic and copies ran while one was open for 1% of the time, Pallas kernels for 0%

commit v1 on v0

--- a/solution.py
+++ b/solution.py
@@ -122,7 +122,7 @@
         0,
     )
     bias_local = jnp.sum(grad_hidden.astype(jnp.float32), 0)
-    small_grads, grad_b_in = lax.psum((small_local, bias_local), ("row", "col"))
+    small_grads, grad_b_in = lax.psum(lax.psum((small_local, bias_local), "col"), "row")
     return (block_out, grad_input, grad_w_in, grad_w_out, small_grads, grad_b_in)
 
 

time: 1690 us -> 2010 us (1.19)
  waiting for transfers between devices: 1540 us -> 1840 us
    psum x0 -> x2, waiting for transfers between devices: none -> 232 us  [the longest x1 232 us: on_device(): lax.psum(lax.psum((small_local, bias_local), 'col'), 'row')]
    unnamed x4 -> x6, waiting for transfers between devices: 178 us -> 249 us
    psum x1 -> x2, blocking collectives: 73.7 us -> 77.6 us  [the longest x1 66.7 us: on_device(): lax.psum(lax.psum((small_local, bias_local), 'col'), 'row')]
  transfers between devices with their start and end apart: 11 -> 13, of which waited for: 7 -> 6; matrix products, arithmetic and copies ran while one was open for 1% -> 1% of each run, Pallas kernels for 0% -> 0%
where the time goes in v1:
time: 2010 us; the launch traced here: 2000 us
  waiting for transfers between devices  1840 us (92%)
  blocking collectives  77.6 us (4%)
  starting transfers between devices  24.2 us (1%)
  local copies, waits for them, and re-layouts  21.1 us (1%)
    all_gather x1, waiting for transfers between devices, on_device(): w_out_full = lax.all_gather(w_out, ('row', 'col'), axis=0, tiled=True)  684 us
    all_gather x1, waiting for transfers between devices, on_device(): w_in_full = lax.all_gather(w_in, ('row', 'col'), axis=1, tiled=True)  672 us
    unnamed x6, waiting for transfers between devices  249 us
    psum x1, waiting for transfers between devices, on_device(): lax.psum(lax.psum((small_local, bias_local), 'col'), 'row')  232 us
    psum x1, blocking collectives, on_device(): lax.psum(lax.psum((small_local, bias_local), 'col'), 'row')  66.7 us
  transfers between devices with their start and end apart: 13, of which 6 were waited for; matrix products, arithmetic and copies ran while one was open for 1% of the time, Pallas kernels for 0%

profile of v1, /device:TPU:99, one launch (start us, length us, event | category | flops | bytes accessed | tf_op | source)
XLA Modules:
  0.0 2002.8 jit_solution(13810848243569947845)
XLA Ops:
  7.2 0.0 all-gather.5.cloned.1.call-start
  7.2 0.7 all-gather.5.cloned.1.call-update
  7.9 0.0 all-gather.7.cloned.1.call-start
  7.9 0.9 fusion.63
  8.9 2.6 collective-permute-start.1
  11.5 4.7 collective-permute-start
  16.2 0.0 all-gather.7.cloned.1.call-update
  16.2 0.0 all-reduce.7.cloned.1.call-start
  16.3 1.1 slice_reduce_fusion.47
  17.4 1.0 fusion.56
  18.4 1.2 slice_reduce_fusion.48
  19.7 1.0 constant_dynamic-update-slice_fusion.1
  20.8 3.0 collective-permute-start.2
  23.7 3.2 collective-permute-start.3
  27.0 1.0 slice_reduce_fusion.46
  28.0 0.0 copy-start.39
  28.0 0.0 copy-start.41
  28.0 0.6 broadcast_in_dim.10
  28.6 0.2 collective-permute-done.3
  28.8 0.1 maximum_convert_fusion
  28.9 0.0 copy-start.43
  29.0 3.2 fusion.60
  32.3 0.2 multiply_reduce_fusion.52
  32.5 0.1 add_convert_fusion
  32.7 671.7 %all-gather.5.cloned.1.call-done = bf16[256,6,384]{2,1,0:T(8,128)(2,1)} async-done(((bf16[1,6,384]{2,1,0:T(8,128)(2,1)}), bf16[256,6,384]{2,1,0:T(8,128)(2,1)}) %all-gather.5.cloned.1.call-update) | async-done | bytes 1179664 | tf_op jit(solution)/shard_map/all_gather | solution.py:53
  704.4 2.3 reshape.74
  706.7 2.5 multiply_convert_fusion
  709.2 684.3 %all-gather.7.cloned.1.call-done = bf16[256,6,384]{2,1,0:T(8,128)(2,1)} async-done(((bf16[1,6,384]{2,1,0:T(8,128)(2,1)}), bf16[256,6,384]{2,1,0:T(8,128)(2,1)}) %all-gather.7.cloned.1.call-update) | async-done | bytes 1179664 | tf_op jit(solution)/shard_map/all_gather | solution.py:54
  1393.5 3.3 reshape.76
  1396.8 3.5 fusion.58
  1400.3 0.0 copy-start.44
  1400.3 0.9 convert_reduce_fusion
  1401.3 0.7 fusion.59
  1401.9 0.2 copy-done.5
  1402.1 0.1 div.17
  1402.2 0.2 multiply_reduce_fusion
  1402.5 0.9 multiply_reduce_fusion.1
  1403.4 0.6 multiply_reduce_fusion.37
  1403.9 0.7 multiply_reduce_fusion.19
  1404.7 0.4 copy-done.1
  1405.1 0.0 copy-done.8
  1405.1 2.0 fusion.65
  1407.7 4.4 concatenate.19
  1412.0 0.0 all-reduce.7.cloned.1.call-update
  1412.1 0.0 all-reduce.11.cloned.1.call-start
  1412.1 2.1 fusion.64
  1414.2 0.0 all-reduce.11.cloned.1.call-update
  1414.2 0.0 copy-start.4
  1414.4 0.0 all-reduce.9.cloned.1.call-start
  1414.5 1.9 collective-permute-start.4
  1416.4 2.4 collective-permute-start.5
  1418.9 4.8 collective-permute-done.5
  1423.7 1.9 collective-permute-start.6
  1425.6 4.3 collective-permute-start.7
  1429.9 10.9 psum.30
  1440.7 66.7 %psum.31 = f32[1536]{0:T(1024)} all-reduce(f32[1536]{0:T(1024)S(1)} %psum.30), channel_id=1, replica_groups=mesh['row'=32,'col'=8] {'row'}, use_global_device_ids=true, to_apply=%region_63.0 | all-reduce | flops 1536 | bytes 12288 | tf_op jit(solution)/shard_map/psum | solution.py:125
  1507.4 0.0 all-reduce.9.cloned.1.call-update
  1507.5 0.1 maximum_convert_fusion.1
  1507.8 3.5 fusion.7
  1511.3 248.6 %all-reduce.11.cloned.1.call-done = (f32[384,1536]{0,1:T(8,128)}, f32[1536,384]{1,0:T(8,128)}) async-done(((f32[384,1536]{0,1:T(8,128)}, f32[1536,384]{1,0:T(8,128)}), (f32[384,1536]{0,1:T(8,128)}, f32[1536,384]{1,0:T(8,128)})) %all-reduce.11.cloned.1.call-update) | async-done | bytes 4718608
  1759.9 1.3 constant_dynamic-slice_fusion.1
  1761.2 1.3 constant_dynamic-slice_fusion
  1762.6 232.1 %all-reduce.9.cloned.1.call-done = f32[53,384]{1,0:T(8,128)} async-done(((f32[53,384]{1,0:T(8,128)}), f32[53,384]{1,0:T(8,128)}) %all-reduce.9.cloned.1.call-update) | async-done | bytes 81424 | tf_op jit(solution)/shard_map/psum | solution.py:125
  1994.7 1.5 copy.22
  (156 shorter events, 0.5 us)
Async XLA Ops:
  7.2 697.2 %all-gather.5.cloned.1.call-start = ((), (), s32[]{:S(2)}) async-start(), calls=%async_computation.2 | async-start | bytes 1579008 | tf_op jit(solution)/shard_map/all_gather | solution.py:53
  7.9 1385.6 %all-gather.7.cloned.1.call-start = ((), (), s32[]{:S(2)}) async-start(), calls=%async_computation.3 | async-start | bytes 1579008 | tf_op jit(solution)/shard_map/all_gather | solution.py:54
  8.9 11.8 collective-permute-start.1
  11.5 8.2 collective-permute-start
  16.2 1491.2 %all-reduce.7.cloned.1.call-start = ((), (), s32[]{:S(2)}) async-start(), calls=%async_computation | async-start | bytes 172032 | tf_op jit(solution)/shard_map/psum | solution.py:125
  19.6 12.5 copy-start.9
  19.6 12.5 copy-start.11
  19.6 12.5 copy-start.13
  19.7 12.5 copy-start.15
  19.7 12.5 copy-start.17
  19.7 12.5 copy-start.19
  20.8 7.8 collective-permute-start.2
  23.7 5.1 collective-permute-start.3
  27.9 4.2 copy-start.21
  27.9 4.2 copy-start.23
  27.9 4.2 copy-start.25
  28.0 4.2 copy-start.27
  28.0 4.2 copy-start.29
  28.0 4.2 copy-start.31
  28.0 4.2 copy-start.33
  28.0 4.2 copy-start.35
  28.0 4.2 copy-start.37
  28.0 4.2 copy-start.39
  28.0 4.2 copy-start.41
  28.9 3.5 copy-start.43
  29.0 3.5 copy-start.46
  709.2 691.1 %copy-start = (bf16[256,1536]{1,0:T(8,128)(2,1)}, bf16[256,1536]{1,0:T(8,128)(2,1)S(1)}, u32[]{:S(2)}) copy-start(bf16[256,1536]{1,0:T(8,128)(2,1)S(1)} %get-tuple-element.125) | copy-start | bytes 2359300
  1396.8 3.5 copy-start.2
  1396.8 3.5 copy-start.3
  1400.3 0.9 copy-start.7
  1400.3 1.0 copy-start.44
  1401.2 0.9 copy-start.5
  1403.9 1.1 copy-start.1
  1403.9 1.2 copy-start.8
  1405.1 2.0 copy-start.47
  1405.1 2.6 copy-start.45
  1405.1 7.0 copy-start.6
  1412.1 347.8 %all-reduce.11.cloned.1.call-start = ((), (), s32[]{:S(2)}) async-start(), calls=%async_computation.4 | async-start | bytes 9437184
  1414.2 93.4 %copy-start.4 = (bf16[8,32,384]{2,1,0:T(8,128)(2,1)S(1)}, bf16[8,32,384]{2,1,0:T(8,128)(2,1)}, u32[]{:S(2)}) copy-start(bf16[8,32,384]{2,1,0:T(8,128)(2,1)} %param.19) | copy-start | bytes 589828
  1414.3 93.4 %copy-start.10 = (f32[384]{0:T(512)S(1)}, f32[384]{0:T(512)}, u32[]{:S(2)}) copy-start(f32[384]{0:T(512)} %copy-done.9) | copy-start | bytes 4612
  1414.3 93.4 %copy-start.12 = (f32[384]{0:T(512)S(1)}, f32[384]{0:T(512)}, u32[]{:S(2)}) copy-start(f32[384]{0:T(512)} %copy-done.11) | copy-start | bytes 4612
  1414.3 93.4 %copy-start.14 = (f32[384]{0:T(512)S(1)}, f32[384]{0:T(512)}, u32[]{:S(2)}) copy-start(f32[384]{0:T(512)} %copy-done.13) | copy-start | bytes 4612
  1414.3 93.4 %copy-start.16 = (f32[384]{0:T(512)S(1)}, f32[384]{0:T(512)}, u32[]{:S(2)}) copy-start(f32[384]{0:T(512)} %copy-done.15) | copy-start | bytes 4612
  1414.3 93.4 %copy-start.18 = (f32[384]{0:T(512)S(1)}, f32[384]{0:T(512)}, u32[]{:S(2)}) copy-start(f32[384]{0:T(512)} %copy-done.17) | copy-start | bytes 4612
  1414.3 93.4 %copy-start.20 = (f32[384]{0:T(512)S(1)}, f32[384]{0:T(512)}, u32[]{:S(2)}) copy-start(f32[384]{0:T(512)} %copy-done.19) | copy-start | bytes 4612
  1414.3 93.4 %copy-start.22 = (f32[384]{0:T(512)S(1)}, f32[384]{0:T(512)}, u32[]{:S(2)}) copy-start(f32[384]{0:T(512)} %copy-done.21) | copy-start | bytes 4612
  1414.3 93.4 %copy-start.24 = (f32[384]{0:T(512)S(1)}, f32[384]{0:T(512)}, u32[]{:S(2)}) copy-start(f32[384]{0:T(512)} %copy-done.23) | copy-start | bytes 4612
  1414.3 93.4 %copy-start.26 = (f32[384]{0:T(512)S(1)}, f32[384]{0:T(512)}, u32[]{:S(2)}) copy-start(f32[384]{0:T(512)} %copy-done.25) | copy-start | bytes 4612
  1414.3 93.4 %copy-start.28 = (f32[384]{0:T(512)S(1)}, f32[384]{0:T(512)}, u32[]{:S(2)}) copy-start(f32[384]{0:T(512)} %copy-done.27) | copy-start | bytes 4612
  1414.4 93.4 %copy-start.30 = (f32[384]{0:T(512)S(1)}, f32[384]{0:T(512)}, u32[]{:S(2)}) copy-start(f32[384]{0:T(512)} %copy-done.29) | copy-start | bytes 4612
  1414.4 93.4 %copy-start.32 = (f32[384]{0:T(512)S(1)}, f32[384]{0:T(512)}, u32[]{:S(2)}) copy-start(f32[384]{0:T(512)} %copy-done.31) | copy-start | bytes 4612
  1414.4 93.4 %copy-start.34 = (f32[384]{0:T(512)S(1)}, f32[384]{0:T(512)}, u32[]{:S(2)}) copy-start(f32[384]{0:T(512)} %copy-done.33) | copy-start | bytes 4612
  1414.4 93.4 %copy-start.36 = (f32[384]{0:T(512)S(1)}, f32[384]{0:T(512)}, u32[]{:S(2)}) copy-start(f32[384]{0:T(512)} %copy-done.35) | copy-start | bytes 4612
  1414.4 93.4 %copy-start.38 = (f32[384]{0:T(512)S(1)}, f32[384]{0:T(512)}, u32[]{:S(2)}) copy-start(f32[384]{0:T(512)} %copy-done.37) | copy-start | bytes 4612
  1414.4 93.4 %copy-start.40 = (f32[384]{0:T(512)S(1)}, f32[384]{0:T(512)}, u32[]{:S(2)}) copy-start(f32[384]{0:T(512)} %copy-done.39) | copy-start | bytes 4612
  1414.4 93.4 %copy-start.42 = (f32[384]{0:T(512)S(1)}, f32[384]{0:T(512)}, u32[]{:S(2)}) copy-start(f32[384]{0:T(512)} %copy-done.41) | copy-start | bytes 4612
  1414.4 580.3 %all-reduce.9.cloned.1.call-start = ((), (), s32[]{:S(2)}) async-start(), calls=%async_computation.1 | async-start | bytes 172032 | tf_op jit(solution)/shard_map/psum | solution.py:125
  1414.5 4.3 collective-permute-start.4
  1416.4 7.2 collective-permute-start.5
  1423.7 83.8 %collective-permute-start.6 = (bf16[14,3,384]{2,1,0:T(4,128)(2,1)S(1)}, bf16[14,3,384]{2,1,0:T(4,128)(2,1)S(1)}, u32[]{:S(2)}, u32[]{:S(2)}) collective-permute-start(bf16[14,3,384]{2,1,0:T(4,128)(2,1)S(1)} %get-tuple-element.116), channel_id=1, source_target_pairs={{0,1},{1,2},{2,3},{3,4},{4,5},{5,6},{6,7},{8,9},{9,10},{10,11},{11... | collective-permute-start | bytes 96776 | tf_op jit(solution)/shard_map/ppermute | solution.py:15
  1425.6 81.9 %collective-permute-start.7 = (bf16[14,3,384]{2,1,0:T(4,128)(2,1)S(1)}, bf16[14,3,384]{2,1,0:T(4,128)(2,1)S(1)}, u32[]{:S(2)}, u32[]{:S(2)}) collective-permute-start(bf16[14,3,384]{2,1,0:T(4,128)(2,1)S(1)} %get-tuple-element.117), channel_id=1, source_target_pairs={{1,0},{2,1},{3,2},{4,3},{5,4},{6,5},{7,6},{9,8},{10,9},{11,10},{12... | collective-permute-start | bytes 96776 | tf_op jit(solution)/shard_map/ppermute | solution.py:16
Sparse Core Ops, SparseCore 0:
  9.9 694.4 all-gather.4
  706.2 687.2 all-gather.6
  1412.2 63.9 all-reduce.6
  1482.5 277.3 all-reduce.10
  1762.4 232.2 all-reduce.8
